TPU v7x, 32 devices: a whole 2x2x4 slice. The times are simulated.
32 devices in a mesh: grp: 2 (over y), seq: 4 (over z), req: 2 (over x), hd: 2 (over core).
Axes of the slice: x: 2, y: 2, z: 4, core: 2. Of those that a mesh axis runs over, the one named last changes fastest.
Arguments:
- cache: bfloat16 [8, 8, 1536, 256], P(('grp', 'req'), 'hd', 'seq'), parts along dimension 0, may hold values from -7 to 7
- evicted: bfloat16 [8, 8, 256, 256], P(('grp', 'req'), 'hd', 'seq'), parts along dimension 0, may hold values from -6 to 6
- merge_weight: bfloat16 [8, 8, 256], P(('grp', 'req'), 'hd', 'seq'), parts along dimension 0, may hold values from 0.25 to 2.5
- targets: int32 [8, 8, 256], P(('grp', 'req'), 'hd', 'seq'), parts along dimension 0, may hold values from 0 to 1535, as said below
- kept_counts: int32 [8, 4], P(('grp', 'req'), 'seq'), parts along dimension 0, may hold values from 192 to 384, as said below
- queries: bfloat16 [4, 8, 64, 128], P(None, ('grp', 'req'), 'hd'), parts along dimension 1, may hold values from -1024 to 1024
- new_rows: bfloat16 [4, 8, 8, 256], P(None, ('grp', 'req'), 'hd'), parts along dimension 1, may hold values from -8 to 8
Outputs:
- merged_cache: bfloat16 [8, 8, 1536, 256], P(('grp', 'req'), 'hd', 'seq'), parts along dimension 0
- attended: bfloat16 [4, 8, 64, 128], P(None, ('grp', 'req'), 'hd'), parts along dimension 1
There are 2 independent parts, one for each index of `grp`. A program takes and returns all parts, laid end to end along the dimension named above; each array names one. Nothing has to cross between parts.
Inputs may be any that keep to these rules, and one draw needn't show every extreme that they name: `targets`: for each request, head and block of 64 evicted rows, at most 32 rows target one block of 384 kept positions; every target is a live position. `kept_counts`: each request has a block with all 384 positions live.
All inputs are finite; a program needn't handle non-finite values.
Results may differ from a plain program's by a relative error of at most 0.0029.
Values may be sent and summed in bfloat16 or wider, within the bound.
A program may use at most 64 MiB of HBM per device.

v0:
```python
import functools
import math

import jax
import jax.numpy as jnp
from jax import lax
from jax.experimental import pallas as pl
from jax.experimental.pallas import tpu as pltpu
from jax.sharding import PartitionSpec as P

F32 = jnp.float32
BF16 = jnp.bfloat16
NEG = -1e30


def contract_last(a, b):
    return lax.dot_general(a, b, (((1,), (1,)), ((), ())), preferred_element_type=F32)


def softmax_block(query, keys, values, allowed, scale):
    scores = jnp.where(allowed, contract_last(query, keys) * scale, NEG)
    highest = jnp.max(scores, axis=-1, keepdims=True)
    exponent = jnp.exp(scores - highest)
    total = jnp.sum(exponent, axis=-1, keepdims=True)
    weighted = jnp.dot(exponent.astype(BF16), values, preferred_element_type=F32)
    return highest, total, weighted


def kernel(
    shards, cap, groups, owners,
    cache, evicted, weight, target, counts, queries, fresh,
    merged, attended,
    evict_v, weight_v, target_v, counts_v, query_v, fresh_v,
    send, recv, meta_send, meta_recv, query_s, fresh_o, fresh_ml,
    part, part_recv, result,
    in_sem, cache_sem, row_ssem, row_rsem, meta_ssem, meta_rsem,
    part_ssem, part_rsem, res_ssem, res_rsem,
):
    reqs, heads, kept, width = merged.shape
    pairs = reqs * heads
    evict = evict_v.shape[2]
    steps, _, _, depth = query_v.shape
    rows = query_s.shape[1]
    group = rows // steps
    slots = shards * cap
    per = pairs // owners
    scale = 1.0 / math.sqrt(depth)
    me = lax.axis_index("seq")

    def peer(d):
        return lax.rem(me + d, shards)

    def source(d):
        return lax.rem(me + shards - d, shards)

    def remote(src, dst, ssem, rsem, device):
        return pltpu.make_async_remote_copy(
            src_ref=src, dst_ref=dst, send_sem=ssem, recv_sem=rsem,
            device_id={"seq": device}, device_id_type=pl.DeviceIdType.MESH,
        )

    small = [
        pltpu.make_async_copy(src, dst, in_sem.at[i])
        for i, (src, dst) in enumerate((
            (target, target_v), (weight, weight_v), (evicted, evict_v),
            (queries, query_v), (fresh, fresh_v), (counts, counts_v),
        ))
    ]
    for copy in small:
        copy.start()
    order = []
    for o in [0] + list(range(owners - 1, 0, -1)):
        order += [o * per + j for j in range(per)]
    loads = {}
    for i in order:
        r, h = divmod(i, heads)
        loads[i] = pltpu.make_async_copy(cache.at[r, h], merged.at[r, h], cache_sem.at[i])
        loads[i].start()

    barrier = pltpu.get_barrier_semaphore()
    for d in range(1, shards):
        pl.semaphore_signal(
            barrier, inc=1, device_id={"seq": peer(d)}, device_id_type=pl.DeviceIdType.MESH
        )

    for copy in small[:3]:
        copy.wait()
    aimed = jnp.concatenate([target_v[r] for r in range(reqs)], axis=0)
    weights = jnp.concatenate([weight_v[r].astype(F32) for r in range(reqs)], axis=0)
    owned, position, base = [], jnp.zeros_like(aimed), jnp.zeros(aimed.shape, F32)
    for d in range(shards):
        low = peer(d) * kept
        mine = (aimed >= low) & (aimed < low + kept)
        owned.append(jnp.where(mine, 1.0, 0.0))
        position = jnp.where(mine, aimed - low, position)
        base = jnp.where(mine, float(d * cap), base)
    above = lax.broadcasted_iota(jnp.int32, (evict, evict), 0) < lax.broadcasted_iota(
        jnp.int32, (evict, evict), 1
    )
    earlier = jnp.dot(
        jnp.concatenate(owned, axis=0).astype(BF16),
        jnp.where(above, 1.0, 0.0).astype(BF16),
        preferred_element_type=F32,
    )
    slot = base
    for d in range(shards):
        slot = slot + owned[d] * earlier[d * pairs : (d + 1) * pairs]
    slot = slot.astype(jnp.int32)
    features = jnp.concatenate(
        [weights, (position & 255).astype(F32), (position >> 8).astype(F32)], axis=0
    ).astype(BF16)
    slot_row = lax.broadcasted_iota(jnp.int32, (slots, evict), 0)
    for i in order:
        r, h = divmod(i, heads)
        packing = jnp.where(slot_row == slot[i : i + 1, :], 1.0, 0.0).astype(BF16)
        packed = jnp.dot(packing, evict_v[r, h], preferred_element_type=F32).astype(BF16)
        send[i] = packed
        recv[i, 0:cap, :] = packed[0:cap]
        meta = contract_last(features, packing)
        meta_send[i : i + 1, :] = meta[i : i + 1]
        meta_send[pairs + i : pairs + i + 1, :] = (
            meta[2 * pairs + i : 2 * pairs + i + 1] * 256.0 + meta[pairs + i : pairs + i + 1]
        )

    pl.semaphore_wait(barrier, shards - 1)

    meta_copies = {}
    for d in range(1, shards):
        meta_copies[d] = remote(
            meta_send, meta_recv.at[d], meta_ssem.at[d], meta_rsem.at[d], peer(d)
        )
        meta_copies[d].start()
    span = pairs // groups
    row_copies = {}
    for g in range(groups):
        first = order[g] if groups == pairs else g * span
        for d in range(1, shards):
            lot = (pl.ds(first, span), pl.ds(d * cap, cap))
            row_copies[first, d] = remote(
                send.at[lot], recv.at[lot], row_ssem.at[g, d], row_rsem.at[g, d], peer(d)
            )
            row_copies[first, d].start()

    for copy in small[3:]:
        copy.wait()
    diagonal = lax.broadcasted_iota(jnp.int32, (rows, 128), 0) == lax.broadcasted_iota(
        jnp.int32, (rows, 128), 1
    )

    def to_rows(*columns):
        flat = [jnp.sum(jnp.where(diagonal, c, 0.0), axis=0, keepdims=True) for c in columns]
        return jnp.concatenate(flat + [jnp.zeros((8 - len(flat), 128), F32)], axis=0)

    def to_column(row):
        return jnp.sum(jnp.where(diagonal, row, 0.0), axis=1, keepdims=True)

    padded = -(-steps // 16) * 16
    new_step = lax.broadcasted_iota(jnp.int32, (rows, padded), 1)
    row_index = lax.broadcasted_iota(jnp.int32, (rows, padded), 0)
    allowed = row_index < 0
    for s in range(steps):
        allowed = allowed | ((new_step == s) & (row_index >= s * group))
    for r in range(reqs):
        asked = [query_v[s, r].astype(F32) for s in range(steps)]
        added = [fresh_v[s, r].astype(F32) for s in range(steps)]
        for h in range(heads):
            i = r * heads + h
            query = jnp.concatenate(
                [a[h * group : (h + 1) * group] for a in asked], axis=0
            ).astype(BF16)
            query_s[i] = query
            latest = jnp.concatenate(
                [a[h : h + 1] for a in added] + [jnp.zeros((padded - steps, width), F32)], axis=0
            ).astype(BF16)
            highest, total, weighted = softmax_block(
                query, latest[:, :depth], latest[:, depth:], allowed, scale
            )
            fresh_o[i] = weighted
            fresh_ml[i] = to_rows(highest, total)

    for d in range(1, shards):
        meta_copies[d].wait_recv()
    lane = lax.broadcasted_iota(jnp.int32, (2 * pairs, slots), 1)
    meta = meta_send[...]
    for d in range(1, shards):
        meta = jnp.where(lane >= d * cap, meta_recv[d], meta)
    slot_weight = meta[:pairs]
    slot_position = meta[pairs:].astype(jnp.int32)

    kept_row = lax.broadcasted_iota(jnp.int32, (kept, slots), 0)
    kept_lane = lax.broadcasted_iota(jnp.int32, (rows, kept), 1)
    ones = jnp.ones((slots, 128), BF16)
    for n, i in enumerate(order):
        r, h = divmod(i, heads)
        loads[i].wait()
        if groups == pairs:
            for d in range(1, shards):
                row_copies[i, d].wait_recv()
        elif n == 0:
            for copy in row_copies.values():
                copy.wait_recv()
        placing = jnp.where(
            kept_row == slot_position[i : i + 1], slot_weight[i : i + 1], 0.0
        ).astype(BF16)
        summed = jnp.dot(placing, recv[i], preferred_element_type=F32)
        factor = 1.0 / (1.0 + jnp.dot(placing, ones, preferred_element_type=F32))
        factor = jnp.concatenate([factor] * (width // 128), axis=1)
        fused = ((merged[r, h].astype(F32) + summed) * factor).astype(BF16)
        merged[r, h] = fused
        highest, total, weighted = softmax_block(
            query_s[i], fused[:, :depth], fused[:, depth:], kept_lane < counts_v[:, r : r + 1], scale
        )
        part[i, 0:rows, :] = weighted
        part[i, rows : rows + 8, :] = to_rows(highest, total)
        owner, j = divmod(i, per)
        away = lax.rem(owner - me + shards, shards)

        @pl.when(me != owner)
        def _():
            remote(
                part.at[i], part_recv.at[j, away], part_ssem.at[i], part_rsem.at[j, away], owner
            ).start()

    def part_in(j, d):
        return remote(
            part.at[j], part_recv.at[j, d], part_ssem.at[j], part_rsem.at[j, d], peer(d)
        )

    def res_out(j, d):
        mine = me * per + j
        return remote(
            result.at[mine], result.at[mine], res_ssem.at[j, d], res_rsem.at[j, d], peer(d)
        )

    def res_in(j, d):
        theirs = source(d) * per + j
        return remote(
            result.at[theirs], result.at[theirs], res_ssem.at[j, d], res_rsem.at[j, d], peer(d)
        )

    def only_owners(index, f):
        if owners == shards:
            f()
        else:
            pl.when(index < owners)(f)

    def combine():
        for j in range(per):
            mine = me * per + j
            for d in range(1, shards):
                part_in(j, d).wait_recv()
            tiles = [fresh_ml[mine], part[mine, rows : rows + 8, :]]
            outs = [fresh_o[mine], part[mine, 0:rows, :]]
            for d in range(1, shards):
                tiles.append(part_recv[j, d, rows : rows + 8, :])
                outs.append(part_recv[j, d, 0:rows, :])
            top = tiles[0][0:1]
            for tile in tiles[1:]:
                top = jnp.maximum(top, tile[0:1])
            shares = [jnp.exp(tile[0:1] - top) for tile in tiles]
            total = shares[0] * tiles[0][1:2]
            for share, tile in zip(shares[1:], tiles[1:]):
                total = total + share * tile[1:2]
            lanes = lax.broadcasted_iota(jnp.int32, total.shape, 1)
            total = jnp.where(lanes < rows, total, 1.0)
            blend = to_column(shares[0] / total) * outs[0]
            for share, out in zip(shares[1:], outs[1:]):
                blend = blend + to_column(share / total) * out
            result[mine] = blend.astype(BF16)
            for d in range(1, shards):
                res_out(j, d).start()

    only_owners(me, combine)

    for j in range(per):
        for d in range(1, shards):
            only_owners(source(d), lambda: res_in(j, d).wait_recv())
    for r in range(reqs):
        done = [result[r * heads + h].astype(F32) for h in range(heads)]
        for s in range(steps):
            attended[s, r] = jnp.concatenate(
                [a[s * group : (s + 1) * group] for a in done], axis=0
            ).astype(BF16)

    for copy in list(meta_copies.values()) + list(row_copies.values()):
        copy.wait_send()
    for i in order:
        owner = i // per

        @pl.when(me != owner)
        def _():
            remote(
                part.at[i], part_recv.at[0, 1], part_ssem.at[i], part_rsem.at[0, 1], owner
            ).wait_send()

    def drain():
        for j in range(per):
            for d in range(1, shards):
                res_out(j, d).wait_send()

    only_owners(me, drain)


def write_out(merged, attended, merged_out, attended_out, sem):
    copies = [
        pltpu.make_async_copy(merged, merged_out, sem.at[0]),
        pltpu.make_async_copy(attended, attended_out, sem.at[1]),
    ]
    for copy in copies:
        copy.start()
    for copy in copies:
        copy.wait()


def body(shards, cache, evicted, merge_weight, targets, kept_counts, queries, new_rows):
    reqs, heads, kept, width = cache.shape
    pairs = reqs * heads
    evict = evicted.shape[2]
    steps, _, query_local, depth = queries.shape
    rows = steps * query_local // heads
    cap = -(-max(2, 2 * evict // shards) // 16) * 16
    slots = shards * cap
    groups = pairs if shards <= 8 else 1
    owners = min(shards, pairs)
    per = pairs // owners
    dma = pltpu.SemaphoreType.DMA
    done = pl.pallas_call(
        functools.partial(kernel, shards, cap, groups, owners),
        out_shape=(
            jax.ShapeDtypeStruct(cache.shape, BF16),
            jax.ShapeDtypeStruct(queries.shape, BF16),
        ),
        in_specs=[pl.BlockSpec(memory_space=pltpu.HBM)] * 7,
        out_specs=(pl.BlockSpec(memory_space=pltpu.VMEM),) * 2,
        scratch_shapes=[
            pltpu.VMEM(evicted.shape, BF16),
            pltpu.VMEM(merge_weight.shape, BF16),
            pltpu.VMEM(targets.shape, jnp.int32),
            pltpu.VMEM(kept_counts.shape[::-1], jnp.int32),
            pltpu.VMEM(queries.shape, BF16),
            pltpu.VMEM(new_rows.shape, BF16),
            pltpu.VMEM((pairs, slots, width), BF16),
            pltpu.VMEM((pairs, slots, width), BF16),
            pltpu.VMEM((2 * pairs, slots), F32),
            pltpu.VMEM((shards, 2 * pairs, slots), F32),
            pltpu.VMEM((pairs, rows, depth), BF16),
            pltpu.VMEM((pairs, rows, depth), F32),
            pltpu.VMEM((pairs, 8, 128), F32),
            pltpu.VMEM((pairs, rows + 8, depth), F32),
            pltpu.VMEM((per, shards, rows + 8, depth), F32),
            pltpu.VMEM((pairs, rows, depth), BF16),
            dma((6,)),
            dma((pairs,)),
            dma((groups, shards)),
            dma((groups, shards)),
            dma((shards,)),
            dma((shards,)),
            dma((pairs,)),
            dma((per, shards)),
            dma((per, shards)),
            dma((per, shards)),
        ],
        compiler_params=pltpu.CompilerParams(
            collective_id=0, has_side_effects=True, vmem_limit_bytes=48 * 1024 * 1024
        ),
    )(*(
        pltpu.with_memory_space_constraint(a, pltpu.HBM)
        for a in (cache, evicted, merge_weight, targets, kept_counts.T, queries, new_rows)
    ))
    return pl.pallas_call(
        write_out,
        out_shape=tuple(jax.ShapeDtypeStruct(a.shape, a.dtype) for a in done),
        in_specs=[pl.BlockSpec(memory_space=pltpu.VMEM)] * 2,
        out_specs=(pl.BlockSpec(memory_space=pltpu.HBM),) * 2,
        scratch_shapes=[dma((2,))],
    )(*(pltpu.with_memory_space_constraint(a, pltpu.VMEM) for a in done))


def solution(mesh):
    return jax.shard_map(
        functools.partial(body, mesh.shape["seq"]),
        mesh=mesh,
        in_specs=(
            P(("grp", "req"), "hd", "seq", None),
            P(("grp", "req"), "hd", "seq", None),
            P(("grp", "req"), "hd", "seq"),
            P(("grp", "req"), "hd", "seq"),
            P(("grp", "req"), "seq"),
            P(None, ("grp", "req"), "hd", None),
            P(None, ("grp", "req"), "hd", None),
        ),
        out_specs=(P(("grp", "req"), "hd", "seq", None), P(None, ("grp", "req"), "hd", None)),
        check_vma=False,
    )
```

profile of v0, /device:TPU:0, one launch (start us, length us, event | category | flops | bytes accessed | tf_op | source)
XLA Modules:
  0.0 30.2 jit_solution(2803213368073651645)
XLA Ops:
  0.6 28.4 %shard_map.86 = (bf16[2,4,384,256]{3,2,1,0:T(8,128)(2,1)S(1)}, bf16[4,2,32,128]{3,2,1,0:T(8,128)(2,1)S(1)}) custom-call(bf16[2,4,384,256]{3,2,1,0:T(8,128)(2,1)} %cache.1, bf16[2,4,64,256]{3,2,1,0:T(8,128)(2,1)} %evicted.1, bf16[2,4,64]{2,1,0:T(4,128)(2,1)} %weight.1, s32[2,4,64]{2,1,0:T(4,128)} %target.1, s32[1,2]{1,0:T(1,128)} %bitcast.1, ...), custom_call_target="tpu_custom_call" | custom-call | tf_op jit(solution)/shard_map/pallas_call | solution.py:327
  29.0 1.2 %shard_map.87 = (bf16[2,4,384,256]{3,2,1,0:T(8,128)(2,1)}, bf16[4,2,32,128]{3,2,1,0:T(8,128)(2,1)}) custom-call(bf16[2,4,384,256]{3,2,1,0:T(8,128)(2,1)S(1)} %get-tuple-element.4.merged, bf16[4,2,32,128]{3,2,1,0:T(8,128)(2,1)S(1)} %get-tuple-element.5.attended), custom_call_target="tpu_custom_call" | custom-call | tf_op jit(solution)/shard_map/pallas_call | solution.py:370
where the time goes:
time: 30.3 us; the launch traced here: 30.2 us
  Pallas kernels  29.6 us (98%)
  between operations  0.64 us (2%)
    pallas_call x1, Pallas kernels, body(): pl.pallas_call(functools.partial(kernel, shards, cap, groups, owners), ou...  28.4 us
    pallas_call x1, Pallas kernels, body(): pl.pallas_call(write_out, out_shape=tuple((jax.ShapeDtypeStruct(a.shape,...  1.17 us

commit v1 on v0

v1 whole, which is shorter than its diff:
```python
import functools
import math

import jax
import jax.numpy as jnp
from jax import lax
from jax.experimental import pallas as pl
from jax.experimental.pallas import tpu as pltpu
from jax.sharding import PartitionSpec as P

F32 = jnp.float32
BF16 = jnp.bfloat16
NEG = -1e30


def contract_last(a, b):
    return lax.dot_general(a, b, (((1,), (1,)), ((), ())), preferred_element_type=F32)


def softmax_block(query, keys, values, allowed, scale):
    scores = jnp.where(allowed, contract_last(query, keys) * scale, NEG)
    highest = jnp.max(scores, axis=-1, keepdims=True)
    exponent = jnp.exp(scores - highest)
    total = jnp.sum(exponent, axis=-1, keepdims=True)
    weighted = jnp.dot(exponent.astype(BF16), values, preferred_element_type=F32)
    return highest, total, weighted


def kernel(
    shards, cap, groups, plan,
    cache, evicted, weight, target, counts, queries, fresh,
    merged, attended,
    evict_v, weight_v, target_v, counts_v, query_v, fresh_v,
    send, recv, meta_send, meta_recv, query_s, fresh_o, fresh_ml,
    part, part_m, part_recv, part_m_recv, shared, shared_m, result,
    in_sem, cache_sem, row_ssem, row_rsem, meta_ssem, meta_rsem,
    part_ssem, part_rsem, share_ssem, share_rsem, res_ssem, res_rsem,
):
    reqs, heads, kept, width = merged.shape
    pairs = reqs * heads
    evict = evict_v.shape[2]
    steps, _, _, depth = query_v.shape
    rows = query_s.shape[1]
    group = rows // steps
    slots = shards * cap
    scale = 1.0 / math.sqrt(depth)
    me = lax.axis_index("seq")
    core = lax.axis_index("hd")

    def peer(d):
        return lax.rem(me + d, shards)

    def source(d):
        return lax.rem(me + shards - d, shards)

    def remote(src, dst, ssem, rsem, device):
        return pltpu.make_async_remote_copy(
            src_ref=src, dst_ref=dst, send_sem=ssem, recv_sem=rsem,
            device_id={"seq": device}, device_id_type=pl.DeviceIdType.MESH,
        )

    small = [
        pltpu.make_async_copy(src, dst, in_sem.at[i])
        for i, (src, dst) in enumerate((
            (target, target_v), (weight, weight_v), (evicted, evict_v),
            (queries, query_v), (fresh, fresh_v), (counts, counts_v),
        ))
    ]
    for copy in small:
        copy.start()
    loads = []
    for i in range(pairs):
        r, h = divmod(i, heads)
        loads.append(pltpu.make_async_copy(cache.at[r, h], merged.at[r, h], cache_sem.at[i]))
        loads[i].start()

    barrier = pltpu.get_barrier_semaphore()
    for d in range(1, shards):
        pl.semaphore_signal(
            barrier, inc=1, device_id={"seq": peer(d)}, device_id_type=pl.DeviceIdType.MESH
        )

    diagonal = lax.broadcasted_iota(jnp.int32, (rows, 128), 0) == lax.broadcasted_iota(
        jnp.int32, (rows, 128), 1
    )

    def to_rows(*columns):
        flat = [jnp.sum(jnp.where(diagonal, c, 0.0), axis=0, keepdims=True) for c in columns]
        return jnp.concatenate(flat, axis=0)

    def to_column(row):
        return jnp.sum(jnp.where(diagonal, row, 0.0), axis=1, keepdims=True)

    def attend_new():
        padded = -(-steps // 16) * 16
        new_step = lax.broadcasted_iota(jnp.int32, (rows, padded), 1)
        row_index = lax.broadcasted_iota(jnp.int32, (rows, padded), 0)
        allowed = row_index < 0
        for s in range(steps):
            allowed = allowed | ((new_step == s) & (row_index >= s * group))
        for r in range(reqs):
            asked = [query_v[s, r].astype(F32) for s in range(steps)]
            added = [fresh_v[s, r].astype(F32) for s in range(steps)]
            for h in range(heads):
                i = r * heads + h
                query = jnp.concatenate(
                    [a[h * group : (h + 1) * group] for a in asked], axis=0
                ).astype(BF16)
                query_s[i] = query
                latest = jnp.concatenate(
                    [a[h : h + 1] for a in added] + [jnp.zeros((padded - steps, width), F32)],
                    axis=0,
                ).astype(BF16)
                highest, total, weighted = softmax_block(
                    query, latest[:, :depth], latest[:, depth:], allowed, scale
                )
                fresh_o[i] = weighted
                fresh_ml[i, 0:2, :] = to_rows(highest, total)

    for copy in small[3:]:
        copy.wait()

    @pl.when(core != 0)
    def _():
        attend_new()

    for copy in small[:3]:
        copy.wait()
    aimed = jnp.concatenate([target_v[r] for r in range(reqs)], axis=0)
    weights = jnp.concatenate([weight_v[r].astype(F32) for r in range(reqs)], axis=0)
    owned, position, base = [], jnp.zeros_like(aimed), jnp.zeros(aimed.shape, F32)
    for d in range(shards):
        low = peer(d) * kept
        mine = (aimed >= low) & (aimed < low + kept)
        owned.append(jnp.where(mine, 1.0, 0.0))
        position = jnp.where(mine, aimed - low, position)
        base = jnp.where(mine, float(d * cap), base)
    above = lax.broadcasted_iota(jnp.int32, (evict, evict), 0) < lax.broadcasted_iota(
        jnp.int32, (evict, evict), 1
    )
    earlier = jnp.dot(
        jnp.concatenate(owned, axis=0).astype(BF16),
        jnp.where(above, 1.0, 0.0).astype(BF16),
        preferred_element_type=F32,
    )
    slot = base
    for d in range(shards):
        slot = slot + owned[d] * earlier[d * pairs : (d + 1) * pairs]
    slot = slot.astype(jnp.int32)
    features = jnp.concatenate(
        [weights, (position & 255).astype(F32), (position >> 8).astype(F32)], axis=0
    ).astype(BF16)
    slot_row = lax.broadcasted_iota(jnp.int32, (slots, evict), 0)
    for i in range(pairs):
        r, h = divmod(i, heads)
        packing = jnp.where(slot_row == slot[i : i + 1, :], 1.0, 0.0).astype(BF16)
        packed = jnp.dot(packing, evict_v[r, h], preferred_element_type=F32).astype(BF16)
        send[i] = packed
        recv[i, 0:cap, :] = packed[0:cap]
        meta = contract_last(features, packing)
        meta_send[i : i + 1, :] = (
            (meta[2 * pairs + i : 2 * pairs + i + 1] * 256.0 + meta[pairs + i : pairs + i + 1])
            * 2048.0 + meta[i : i + 1] * 512.0
        )

    pl.semaphore_wait(barrier, shards - 1)

    meta_copies = {}
    for d in range(1, shards):
        meta_copies[d] = remote(
            meta_send, meta_recv.at[d], meta_ssem.at[d], meta_rsem.at[d], peer(d)
        )
        meta_copies[d].start()
    span = pairs // groups
    row_copies = {}
    for g in range(groups):
        for d in range(1, shards):
            lot = (pl.ds(g * span, span), pl.ds(d * cap, cap))
            row_copies[g, d] = remote(
                send.at[lot], recv.at[lot], row_ssem.at[g, d], row_rsem.at[g, d], peer(d)
            )
            row_copies[g, d].start()

    @pl.when(core == 0)
    def _():
        attend_new()

    for d in range(1, shards):
        meta_copies[d].wait_recv()
    lane = lax.broadcasted_iota(jnp.int32, (pairs, slots), 1)
    meta = meta_send[...]
    for d in range(1, shards):
        meta = jnp.where(lane >= d * cap, meta_recv[d], meta)
    slot_position = (meta * (1.0 / 2048.0)).astype(jnp.int32)
    slot_weight = (meta - slot_position.astype(F32) * 2048.0) * (1.0 / 512.0)

    kept_row = lax.broadcasted_iota(jnp.int32, (kept, slots), 0)
    kept_lane = lax.broadcasted_iota(jnp.int32, (rows, kept), 1)
    ones = jnp.ones((slots, 128), BF16)

    def merge(i):
        r, h = divmod(i, heads)
        loads[i].wait()
        if groups == pairs:
            for d in range(1, shards):
                row_copies[i, d].wait_recv()
        elif i == 0:
            for copy in row_copies.values():
                copy.wait_recv()
        placing = jnp.where(
            kept_row == slot_position[i : i + 1], slot_weight[i : i + 1], 0.0
        ).astype(BF16)
        summed = jnp.dot(placing, recv[i], preferred_element_type=F32)
        factor = 1.0 / (1.0 + jnp.dot(placing, ones, preferred_element_type=F32))
        factor = jnp.concatenate([factor] * (width // 128), axis=1)
        fused = ((merged[r, h].astype(F32) + summed) * factor).astype(BF16)
        merged[r, h] = fused
        return softmax_block(
            query_s[i], fused[:, :depth], fused[:, depth:], kept_lane < counts_v[:, r : r + 1], scale
        )

    def part_pair(k, count, away, device):
        lot = pl.ds(0, count * rows)
        return (
            remote(
                part.at[k, lot], part_recv.at[k, away, lot],
                part_ssem.at[k, 0], part_rsem.at[k, away, 0], device,
            ),
            remote(
                part_m.at[k], part_m_recv.at[k, away],
                part_ssem.at[k, 1], part_rsem.at[k, away, 1], device,
            ),
        )

    def share_pair(k, count, origin, d):
        lot = shared.at[k, origin, pl.ds(0, count * rows)]
        top = shared_m.at[k, origin]
        return (
            remote(lot, lot, share_ssem.at[k, d, 0], share_rsem.at[k, d, 0], peer(d)),
            remote(top, top, share_ssem.at[k, d, 1], share_rsem.at[k, d, 1], peer(d)),
        )

    def to_owner(k, count, owner):
        return part_pair(k, count, lax.rem(owner - me + shards, shards), owner)

    def send_result(k, first, count, d):
        lot = result.at[pl.ds(first, count)]
        return remote(lot, lot, res_ssem.at[k, d], res_rsem.at[k], peer(d))

    owned_plan = [(k, *entry) for k, entry in enumerate(plan) if entry[2] is not None]
    owned_index = {entry[0]: n for n, entry in enumerate(owned_plan)}
    shared_plan = [(k, *entry) for k, entry in enumerate(plan) if entry[2] is None]
    shared_index = {entry[0]: n for n, entry in enumerate(shared_plan)}

    for k, (first, count, owner) in enumerate(plan):
        for j in range(count):
            highest, total, weighted = merge(first + j)
            size = jnp.maximum(jnp.max(jnp.abs(weighted), axis=-1, keepdims=True), 1e-30)
            coded = jnp.round(weighted * (32767.0 / size)).astype(jnp.int32).astype(jnp.int16)
            if owner is None:
                into, into_m = shared.at[shared_index[k], me], shared_m.at[shared_index[k], me]
            else:
                into, into_m = part.at[owned_index[k]], part_m.at[owned_index[k]]
            into[j * rows : (j + 1) * rows, :] = coded
            into_m[3 * j : 3 * j + 3, :] = to_rows(highest, total, size * (1.0 / 32767.0))
        if owner is None:
            for d in range(1, shards):
                for copy in share_pair(shared_index[k], count, me, d):
                    copy.start()
        else:
            @pl.when(me != owner)
            def _():
                for copy in to_owner(owned_index[k], count, owner):
                    copy.start()

    lanes = lax.broadcasted_iota(jnp.int32, (1, 128), 1)

    def combine(first, count, blocks):
        for j in range(count):
            i = first + j
            tiles = [fresh_ml[i, 0:2, :]] + [m[3 * j : 3 * j + 3, :] for _, m in blocks]
            outs = [fresh_o[i]] + [
                b[j * rows : (j + 1) * rows, :].astype(jnp.int32).astype(F32) for b, _ in blocks
            ]
            top = tiles[0][0:1]
            for tile in tiles[1:]:
                top = jnp.maximum(top, tile[0:1])
            shares = [jnp.exp(tile[0:1] - top) for tile in tiles]
            total = shares[0] * tiles[0][1:2]
            for share, tile in zip(shares[1:], tiles[1:]):
                total = total + share * tile[1:2]
            total = jnp.where(lanes < rows, total, 1.0)
            blend = to_column(shares[0] / total) * outs[0]
            for share, tile, out in zip(shares[1:], tiles[1:], outs[1:]):
                blend = blend + to_column(share * tile[2:3] / total) * out
            result[i] = blend.astype(BF16)

    for k, first, count, owner in owned_plan:
        n = owned_index[k]

        @pl.when(me == owner)
        def _():
            for d in range(1, shards):
                for copy in part_pair(n, count, d, peer(d)):
                    copy.wait_recv()
            combine(
                first, count,
                [(part.at[n], part_m.at[n])]
                + [(part_recv.at[n, d], part_m_recv.at[n, d]) for d in range(1, shards)],
            )
            for d in range(1, shards):
                send_result(n, first, count, d).start()

    for k, first, count, _ in shared_plan:
        n = shared_index[k]
        for d in range(1, shards):
            for copy in share_pair(n, count, source(d), d):
                copy.wait_recv()
        combine(first, count, [(shared.at[n, d], shared_m.at[n, d]) for d in range(shards)])

    for k, first, count, owner in owned_plan:
        @pl.when(me != owner)
        def _():
            send_result(owned_index[k], first, count, 1).wait_recv()

    for r in range(reqs):
        done = [result[r * heads + h].astype(F32) for h in range(heads)]
        for s in range(steps):
            attended[s, r] = jnp.concatenate(
                [a[s * group : (s + 1) * group] for a in done], axis=0
            ).astype(BF16)

    for copy in list(meta_copies.values()) + list(row_copies.values()):
        copy.wait_send()
    for k, first, count, owner in owned_plan:
        n = owned_index[k]

        @pl.when(me != owner)
        def _():
            for copy in to_owner(n, count, owner):
                copy.wait_send()

        @pl.when(me == owner)
        def _():
            for d in range(1, shards):
                send_result(n, first, count, d).wait_send()

    for k, first, count, _ in shared_plan:
        for d in range(1, shards):
            for copy in share_pair(shared_index[k], count, me, d):
                copy.wait_send()


def write_out(merged, attended, merged_out, attended_out, sem):
    copies = [
        pltpu.make_async_copy(merged, merged_out, sem.at[0]),
        pltpu.make_async_copy(attended, attended_out, sem.at[1]),
    ]
    for copy in copies:
        copy.start()
    for copy in copies:
        copy.wait()


def schedule(shards, pairs):
    per = max(1, pairs // shards)
    firsts = list(range(0, pairs, per))
    late = len(firsts) // 2 if shards <= 8 else 0
    return tuple(
        (first, min(per, pairs - first), None)
        if n >= len(firsts) - late
        else (first, min(per, pairs - first), (shards // 2 - 1 + n) % shards)
        for n, first in enumerate(firsts)
    )


def body(shards, cache, evicted, merge_weight, targets, kept_counts, queries, new_rows):
    reqs, heads, kept, width = cache.shape
    pairs = reqs * heads
    evict = evicted.shape[2]
    steps, _, query_local, depth = queries.shape
    rows = steps * query_local // heads
    cap = -(-max(2, 2 * evict // shards) // 16) * 16
    slots = shards * cap
    groups = pairs if shards <= 8 else 1
    plan = schedule(shards, pairs)
    most = max(count for _, count, _ in plan)
    owned = max(1, sum(owner is not None for _, _, owner in plan))
    common = max(1, len(plan) - owned)
    high = -(-3 * most // 8) * 8
    dma = pltpu.SemaphoreType.DMA
    done = pl.pallas_call(
        functools.partial(kernel, shards, cap, groups, plan),
        out_shape=(
            jax.ShapeDtypeStruct(cache.shape, BF16),
            jax.ShapeDtypeStruct(queries.shape, BF16),
        ),
        in_specs=[pl.BlockSpec(memory_space=pltpu.HBM)] * 7,
        out_specs=(pl.BlockSpec(memory_space=pltpu.VMEM),) * 2,
        scratch_shapes=[
            pltpu.VMEM(evicted.shape, BF16),
            pltpu.VMEM(merge_weight.shape, BF16),
            pltpu.VMEM(targets.shape, jnp.int32),
            pltpu.VMEM(kept_counts.shape[::-1], jnp.int32),
            pltpu.VMEM(queries.shape, BF16),
            pltpu.VMEM(new_rows.shape, BF16),
            pltpu.VMEM((pairs, slots, width), BF16),
            pltpu.VMEM((pairs, slots, width), BF16),
            pltpu.VMEM((pairs, slots), F32),
            pltpu.VMEM((shards, pairs, slots), F32),
            pltpu.VMEM((pairs, rows, depth), BF16),
            pltpu.VMEM((pairs, rows, depth), F32),
            pltpu.VMEM((pairs, 8, 128), F32),
            pltpu.VMEM((owned, most * rows, depth), jnp.int16),
            pltpu.VMEM((owned, high, 128), F32),
            pltpu.VMEM((owned, shards, most * rows, depth), jnp.int16),
            pltpu.VMEM((owned, shards, high, 128), F32),
            pltpu.VMEM((common, shards, most * rows, depth), jnp.int16),
            pltpu.VMEM((common, shards, high, 128), F32),
            pltpu.VMEM((pairs, rows, depth), BF16),
            dma((6,)),
            dma((pairs,)),
            dma((groups, shards)),
            dma((groups, shards)),
            dma((shards,)),
            dma((shards,)),
            dma((owned, 2)),
            dma((owned, shards, 2)),
            dma((common, shards, 2)),
            dma((common, shards, 2)),
            dma((owned, shards)),
            dma((owned,)),
        ],
        compiler_params=pltpu.CompilerParams(
            collective_id=0, has_side_effects=True, vmem_limit_bytes=48 * 1024 * 1024
        ),
    )(*(
        pltpu.with_memory_space_constraint(a, pltpu.HBM)
        for a in (cache, evicted, merge_weight, targets, kept_counts.T, queries, new_rows)
    ))
    return pl.pallas_call(
        write_out,
        out_shape=tuple(jax.ShapeDtypeStruct(a.shape, a.dtype) for a in done),
        in_specs=[pl.BlockSpec(memory_space=pltpu.VMEM)] * 2,
        out_specs=(pl.BlockSpec(memory_space=pltpu.HBM),) * 2,
        scratch_shapes=[dma((2,))],
    )(*(pltpu.with_memory_space_constraint(a, pltpu.VMEM) for a in done))


def solution(mesh):
    return jax.shard_map(
        functools.partial(body, mesh.shape["seq"]),
        mesh=mesh,
        in_specs=(
            P(("grp", "req"), "hd", "seq", None),
            P(("grp", "req"), "hd", "seq", None),
            P(("grp", "req"), "hd", "seq"),
            P(("grp", "req"), "hd", "seq"),
            P(("grp", "req"), "seq"),
            P(None, ("grp", "req"), "hd", None),
            P(None, ("grp", "req"), "hd", None),
        ),
        out_specs=(P(("grp", "req"), "hd", "seq", None), P(None, ("grp", "req"), "hd", None)),
        check_vma=False,
    )
```

time: 30.3 us -> 27.3 us (0.901)
  Pallas kernels: 29.6 us -> 26.5 us
    pallas_call x1, Pallas kernels: 28.4 us -> 25.4 us  [body(): pl.pallas_call(functools.partial(kernel, shards, cap, groups, plan), out_...]
where the time goes in v1:
time: 27.3 us; the launch traced here: 27.2 us
  Pallas kernels  26.5 us (97%)
  between operations  0.64 us (2%)
    pallas_call x1, Pallas kernels, body(): pl.pallas_call(functools.partial(kernel, shards, cap, groups, plan), out_...  25.4 us
    pallas_call x1, Pallas kernels, body(): pl.pallas_call(write_out, out_shape=tuple((jax.ShapeDtypeStruct(a.shape,...  1.17 us

profile of v1, /device:TPU:0, one launch (start us, length us, event | category | flops | bytes accessed | tf_op | source)
XLA Modules:
  0.0 27.2 jit_solution(15016132128343824960)
XLA Ops:
  0.6 25.4 %shard_map.86 = (bf16[2,4,384,256]{3,2,1,0:T(8,128)(2,1)S(1)}, bf16[4,2,32,128]{3,2,1,0:T(8,128)(2,1)S(1)}) custom-call(bf16[2,4,384,256]{3,2,1,0:T(8,128)(2,1)} %cache.1, bf16[2,4,64,256]{3,2,1,0:T(8,128)(2,1)} %evicted.1, bf16[2,4,64]{2,1,0:T(4,128)(2,1)} %weight.1, s32[2,4,64]{2,1,0:T(4,128)} %target.1, s32[1,2]{1,0:T(1,128)} %bitcast.1, ...), custom_call_target="tpu_custom_call" | custom-call | tf_op jit(solution)/shard_map/pallas_call | solution.py:392
  26.0 1.2 %shard_map.87 = (bf16[2,4,384,256]{3,2,1,0:T(8,128)(2,1)}, bf16[4,2,32,128]{3,2,1,0:T(8,128)(2,1)}) custom-call(bf16[2,4,384,256]{3,2,1,0:T(8,128)(2,1)S(1)} %get-tuple-element.4.merged, bf16[4,2,32,128]{3,2,1,0:T(8,128)(2,1)S(1)} %get-tuple-element.5.attended), custom_call_target="tpu_custom_call" | custom-call | tf_op jit(solution)/shard_map/pallas_call | solution.py:441

commit v2 on v1

--- a/solution.py
+++ b/solution.py
@@ -33,7 +33,7 @@
     evict_v, weight_v, target_v, counts_v, query_v, fresh_v,
     send, recv, meta_send, meta_recv, query_s, fresh_o, fresh_ml,
     part, part_m, part_recv, part_m_recv, shared, shared_m, result,
-    in_sem, cache_sem, row_ssem, row_rsem, meta_ssem, meta_rsem,
+    in_sem, cache_sem, row_ssem, row_rsem, meta_sem,
     part_ssem, part_rsem, share_ssem, share_rsem, res_ssem, res_rsem,
 ):
     reqs, heads, kept, width = merged.shape
@@ -68,11 +68,8 @@
     ]
     for copy in small:
         copy.start()
-    loads = []
-    for i in range(pairs):
-        r, h = divmod(i, heads)
-        loads.append(pltpu.make_async_copy(cache.at[r, h], merged.at[r, h], cache_sem.at[i]))
-        loads[i].start()
+    load = pltpu.make_async_copy(cache, merged, cache_sem.at[0])
+    load.start()
 
     barrier = pltpu.get_barrier_semaphore()
     for d in range(1, shards):
@@ -165,28 +162,29 @@
 
     pl.semaphore_wait(barrier, shards - 1)
 
-    meta_copies = {}
+    others = pl.ds(1, shards - 1)
+
+    def all_of(ref, ssem, rsem):
+        return remote(ref, ref, ssem, rsem, peer(1))
+
     for d in range(1, shards):
-        meta_copies[d] = remote(
-            meta_send, meta_recv.at[d], meta_ssem.at[d], meta_rsem.at[d], peer(d)
-        )
-        meta_copies[d].start()
+        remote(meta_send, meta_recv.at[d], meta_sem.at[0], meta_sem.at[1], peer(d)).start()
     span = pairs // groups
-    row_copies = {}
     for g in range(groups):
         for d in range(1, shards):
             lot = (pl.ds(g * span, span), pl.ds(d * cap, cap))
-            row_copies[g, d] = remote(
-                send.at[lot], recv.at[lot], row_ssem.at[g, d], row_rsem.at[g, d], peer(d)
-            )
-            row_copies[g, d].start()
+            remote(send.at[lot], recv.at[lot], row_ssem.at[0], row_rsem.at[g], peer(d)).start()
+
+    def rows_in(g):
+        lot = (pl.ds(g * span, span), pl.ds(cap, slots - cap))
+        return all_of(recv.at[lot], row_ssem.at[0], row_rsem.at[g])
 
     @pl.when(core == 0)
     def _():
         attend_new()
 
-    for d in range(1, shards):
-        meta_copies[d].wait_recv()
+    meta_in = all_of(meta_recv.at[others], meta_sem.at[0], meta_sem.at[1])
+    meta_in.wait_recv()
     lane = lax.broadcasted_iota(jnp.int32, (pairs, slots), 1)
     meta = meta_send[...]
     for d in range(1, shards):
@@ -200,13 +198,10 @@
 
     def merge(i):
         r, h = divmod(i, heads)
-        loads[i].wait()
-        if groups == pairs:
-            for d in range(1, shards):
-                row_copies[i, d].wait_recv()
-        elif i == 0:
-            for copy in row_copies.values():
-                copy.wait_recv()
+        if i == 0:
+            load.wait()
+        if i % span == 0:
+            rows_in(i // span).wait_recv()
         placing = jnp.where(
             kept_row == slot_position[i : i + 1], slot_weight[i : i + 1], 0.0
         ).astype(BF16)
@@ -219,33 +214,45 @@
             query_s[i], fused[:, :depth], fused[:, depth:], kept_lane < counts_v[:, r : r + 1], scale
         )
 
-    def part_pair(k, count, away, device):
+    def to_owner(k, count, owner):
         lot = pl.ds(0, count * rows)
+        away = lax.rem(owner - me + shards, shards)
         return (
             remote(
                 part.at[k, lot], part_recv.at[k, away, lot],
-                part_ssem.at[k, 0], part_rsem.at[k, away, 0], device,
+                part_ssem.at[k, 0], part_rsem.at[k, 0], owner,
             ),
             remote(
                 part_m.at[k], part_m_recv.at[k, away],
-                part_ssem.at[k, 1], part_rsem.at[k, away, 1], device,
+                part_ssem.at[k, 1], part_rsem.at[k, 1], owner,
             ),
         )
 
-    def share_pair(k, count, origin, d):
-        lot = shared.at[k, origin, pl.ds(0, count * rows)]
-        top = shared_m.at[k, origin]
+    def parts_in(k, count):
+        lot = pl.ds(0, count * rows)
         return (
-            remote(lot, lot, share_ssem.at[k, d, 0], share_rsem.at[k, d, 0], peer(d)),
-            remote(top, top, share_ssem.at[k, d, 1], share_rsem.at[k, d, 1], peer(d)),
-        )
-
-    def to_owner(k, count, owner):
-        return part_pair(k, count, lax.rem(owner - me + shards, shards), owner)
+            all_of(part_recv.at[k, others, lot], part_ssem.at[k, 0], part_rsem.at[k, 0]),
+            all_of(part_m_recv.at[k, others], part_ssem.at[k, 1], part_rsem.at[k, 1]),
+        )
+
+    def share_rows(k, j, d):
+        lot = shared.at[k, me, pl.ds(j * rows, rows)]
+        return remote(lot, lot, share_ssem.at[k, 0], share_rsem.at[k, 0], peer(d))
+
+    def share_tops(k, d):
+        lot = shared_m.at[k, me]
+        return remote(lot, lot, share_ssem.at[k, 1], share_rsem.at[k, 1], peer(d))
+
+    def shares(k, count):
+        lot = pl.ds(0, count * rows)
+        return (
+            all_of(shared.at[k, others, lot], share_ssem.at[k, 0], share_rsem.at[k, 0]),
+            all_of(shared_m.at[k, others], share_ssem.at[k, 1], share_rsem.at[k, 1]),
+        )
 
     def send_result(k, first, count, d):
         lot = result.at[pl.ds(first, count)]
-        return remote(lot, lot, res_ssem.at[k, d], res_rsem.at[k], peer(d))
+        return remote(lot, lot, res_ssem.at[k], res_rsem.at[k], peer(d))
 
     owned_plan = [(k, *entry) for k, entry in enumerate(plan) if entry[2] is not None]
     owned_index = {entry[0]: n for n, entry in enumerate(owned_plan)}
@@ -262,11 +269,13 @@
             else:
                 into, into_m = part.at[owned_index[k]], part_m.at[owned_index[k]]
             into[j * rows : (j + 1) * rows, :] = coded
+            if owner is None:
+                for d in range(1, shards):
+                    share_rows(shared_index[k], j, d).start()
             into_m[3 * j : 3 * j + 3, :] = to_rows(highest, total, size * (1.0 / 32767.0))
         if owner is None:
             for d in range(1, shards):
-                for copy in share_pair(shared_index[k], count, me, d):
-                    copy.start()
+                share_tops(shared_index[k], d).start()
         else:
             @pl.when(me != owner)
             def _():
@@ -300,9 +309,8 @@
 
         @pl.when(me == owner)
         def _():
-            for d in range(1, shards):
-                for copy in part_pair(n, count, d, peer(d)):
-                    copy.wait_recv()
+            for copy in parts_in(n, count):
+                copy.wait_recv()
             combine(
                 first, count,
                 [(part.at[n], part_m.at[n])]
@@ -313,9 +321,8 @@
 
     for k, first, count, _ in shared_plan:
         n = shared_index[k]
-        for d in range(1, shards):
-            for copy in share_pair(n, count, source(d), d):
-                copy.wait_recv()
+        for copy in shares(n, count):
+            copy.wait_recv()
         combine(first, count, [(shared.at[n, d], shared_m.at[n, d]) for d in range(shards)])
 
     for k, first, count, owner in owned_plan:
@@ -330,8 +337,9 @@
                 [a[s * group : (s + 1) * group] for a in done], axis=0
             ).astype(BF16)
 
-    for copy in list(meta_copies.values()) + list(row_copies.values()):
-        copy.wait_send()
+    meta_in.wait_send()
+    sent = (pl.ds(0, pairs), pl.ds(cap, slots - cap))
+    all_of(recv.at[sent], row_ssem.at[0], row_rsem.at[0]).wait_send()
     for k, first, count, owner in owned_plan:
         n = owned_index[k]
 
@@ -342,13 +350,12 @@
 
         @pl.when(me == owner)
         def _():
-            for d in range(1, shards):
-                send_result(n, first, count, d).wait_send()
+            lot = part_recv.at[n, others, pl.ds(0, count * rows)]
+            all_of(lot, res_ssem.at[n], res_rsem.at[n]).wait_send()
 
     for k, first, count, _ in shared_plan:
-        for d in range(1, shards):
-            for copy in share_pair(shared_index[k], count, me, d):
-                copy.wait_send()
+        for copy in shares(shared_index[k], count):
+            copy.wait_send()
 
 
 def write_out(merged, attended, merged_out, attended_out, sem):
@@ -419,16 +426,15 @@
             pltpu.VMEM((common, shards, high, 128), F32),
             pltpu.VMEM((pairs, rows, depth), BF16),
             dma((6,)),
-            dma((pairs,)),
-            dma((groups, shards)),
-            dma((groups, shards)),
-            dma((shards,)),
-            dma((shards,)),
+            dma((1,)),
+            dma((1,)),
+            dma((groups,)),
+            dma((2,)),
             dma((owned, 2)),
-            dma((owned, shards, 2)),
-            dma((common, shards, 2)),
-            dma((common, shards, 2)),
-            dma((owned, shards)),
+            dma((owned, 2)),
+            dma((common, 2)),
+            dma((common, 2)),
+            dma((owned,)),
             dma((owned,)),
         ],
         compiler_params=pltpu.CompilerParams(

time: 27.3 us -> 26.5 us (0.971)
  Pallas kernels: 26.5 us -> 25.7 us
    pallas_call x1, Pallas kernels: 25.4 us -> 24.5 us  [body(): pl.pallas_call(functools.partial(kernel, shards, cap, groups, plan), out_...]
where the time goes in v2:
time: 26.5 us; the launch traced here: 26.3 us
  Pallas kernels  25.7 us (97%)
  between operations  0.64 us (2%)
    pallas_call x1, Pallas kernels, body(): pl.pallas_call(functools.partial(kernel, shards, cap, groups, plan), out_...  24.5 us
    pallas_call x1, Pallas kernels, body(): pl.pallas_call(write_out, out_shape=tuple((jax.ShapeDtypeStruct(a.shape,...  1.17 us

profile of v2, /device:TPU:0, one launch (start us, length us, event | category | flops | bytes accessed | tf_op | source)
XLA Modules:
  0.0 26.3 jit_solution(8784863352073191137)
XLA Ops:
  0.6 24.5 %shard_map.86 = (bf16[2,4,384,256]{3,2,1,0:T(8,128)(2,1)S(1)}, bf16[4,2,32,128]{3,2,1,0:T(8,128)(2,1)S(1)}) custom-call(bf16[2,4,384,256]{3,2,1,0:T(8,128)(2,1)} %cache.1, bf16[2,4,64,256]{3,2,1,0:T(8,128)(2,1)} %evicted.1, bf16[2,4,64]{2,1,0:T(4,128)(2,1)} %weight.1, s32[2,4,64]{2,1,0:T(4,128)} %target.1, s32[1,2]{1,0:T(1,128)} %bitcast.1, ...), custom_call_target="tpu_custom_call" | custom-call | tf_op jit(solution)/shard_map/pallas_call | solution.py:399
  25.1 1.2 %shard_map.87 = (bf16[2,4,384,256]{3,2,1,0:T(8,128)(2,1)}, bf16[4,2,32,128]{3,2,1,0:T(8,128)(2,1)}) custom-call(bf16[2,4,384,256]{3,2,1,0:T(8,128)(2,1)S(1)} %get-tuple-element.4.merged, bf16[4,2,32,128]{3,2,1,0:T(8,128)(2,1)S(1)} %get-tuple-element.5.attended), custom_call_target="tpu_custom_call" | custom-call | tf_op jit(solution)/shard_map/pallas_call | solution.py:447

commit v3 on v2

--- a/solution.py
+++ b/solution.py
@@ -27,13 +27,13 @@
 
 
 def kernel(
-    shards, cap, groups, plan,
+    shards, cap, chunks, plan,
     cache, evicted, weight, target, counts, queries, fresh,
     merged, attended,
     evict_v, weight_v, target_v, counts_v, query_v, fresh_v,
     send, recv, meta_send, meta_recv, query_s, fresh_o, fresh_ml,
     part, part_m, part_recv, part_m_recv, shared, shared_m, result,
-    in_sem, cache_sem, row_ssem, row_rsem, meta_sem,
+    near_sem, in_sem, cache_sem, row_ssem, row_rsem, meta_sem,
     part_ssem, part_rsem, share_ssem, share_rsem, res_ssem, res_rsem,
 ):
     reqs, heads, kept, width = merged.shape
@@ -71,11 +71,24 @@
     load = pltpu.make_async_copy(cache, merged, cache_sem.at[0])
     load.start()
 
+    def tell(sem, device):
+        pl.semaphore_signal(
+            sem, inc=1, device_id={"seq": device}, device_id_type=pl.DeviceIdType.MESH
+        )
+
+    chain = len(chunks) > 1
     barrier = pltpu.get_barrier_semaphore()
-    for d in range(1, shards):
-        pl.semaphore_signal(
-            barrier, inc=1, device_id={"seq": peer(d)}, device_id_type=pl.DeviceIdType.MESH
-        )
+    if chain:
+        @pl.when(me > 0)
+        def _():
+            tell(barrier, me - 1)
+
+        @pl.when(me < shards - 1)
+        def _():
+            tell(barrier, me + 1)
+    else:
+        for d in range(1, shards):
+            tell(barrier, peer(d))
 
     diagonal = lax.broadcasted_iota(jnp.int32, (rows, 128), 0) == lax.broadcasted_iota(
         jnp.int32, (rows, 128), 1
@@ -148,7 +161,8 @@
         [weights, (position & 255).astype(F32), (position >> 8).astype(F32)], axis=0
     ).astype(BF16)
     slot_row = lax.broadcasted_iota(jnp.int32, (slots, evict), 0)
-    for i in range(pairs):
+
+    def pack(i):
         r, h = divmod(i, heads)
         packing = jnp.where(slot_row == slot[i : i + 1, :], 1.0, 0.0).astype(BF16)
         packed = jnp.dot(packing, evict_v[r, h], preferred_element_type=F32).astype(BF16)
@@ -160,28 +174,98 @@
             * 2048.0 + meta[i : i + 1] * 512.0
         )
 
-    pl.semaphore_wait(barrier, shards - 1)
-
     others = pl.ds(1, shards - 1)
 
     def all_of(ref, ssem, rsem):
         return remote(ref, ref, ssem, rsem, peer(1))
 
-    for d in range(1, shards):
+    def send_rows(c, d):
+        first, count = chunks[c]
+        lot = (pl.ds(first, count), pl.ds(d * cap, cap))
+        remote(send.at[lot], recv.at[lot], row_ssem.at[0], row_rsem.at[c], peer(d)).start()
+
+    def send_meta(d):
         remote(meta_send, meta_recv.at[d], meta_sem.at[0], meta_sem.at[1], peer(d)).start()
-    span = pairs // groups
-    for g in range(groups):
+
+    def rows_in(c):
+        first, count = chunks[c]
+        lot = (pl.ds(first, count), pl.ds(cap, slots - cap))
+        return all_of(recv.at[lot], row_ssem.at[0], row_rsem.at[c])
+
+    def send_rest(m):
+        there = sorted((t for t in range(shards) if t != m), key=lambda t: -abs(t - m))
+        edge = m in (0, shards - 1)
+        for c in range(1, len(chunks)):
+            for t in there[:-1] if edge else there:
+                send_rows(c, (t - m) % shards)
+        if edge:
+            for c in range(1, len(chunks)):
+                send_rows(c, (there[-1] - m) % shards)
+
+    for i in range(chunks[0][1]):
+        pack(i)
+
+    if chain:
+        inner = (me > 0) & (me < shards - 1)
+
+        @pl.when(jnp.logical_not(inner))
+        def _():
+            pl.semaphore_wait(barrier, 1)
+
+        @pl.when(inner)
+        def _():
+            pl.semaphore_wait(barrier, 2)
+            tell(near_sem.at[0, 0], me - 1)
+            tell(near_sem.at[1, 0], me + 1)
+
+        @pl.when(me < shards - 1)
+        def _():
+            send_rows(0, 1)
+
+        @pl.when(me > 0)
+        def _():
+            send_rows(0, shards - 1)
+
+    for i in range(chunks[0][1], pairs):
+        pack(i)
+
+    if chain:
+        @pl.when(core == 0)
+        def _():
+            attend_new()
+
+        for m in range(shards):
+            @pl.when(me == m)
+            def _():
+                for far in range(2, shards):
+                    if m + far < shards:
+                        pl.semaphore_wait(near_sem.at[0, far - 2], 1)
+                        if m > 0:
+                            tell(near_sem.at[0, far - 1], m - 1)
+                        send_rows(0, far)
+                    if m - far >= 0:
+                        pl.semaphore_wait(near_sem.at[1, far - 2], 1)
+                        if m < shards - 1:
+                            tell(near_sem.at[1, far - 1], m + 1)
+                        send_rows(0, shards - far)
+                there = sorted((t for t in range(shards) if t != m), key=lambda t: -abs(t - m))
+                for t in there:
+                    send_meta((t - m) % shards)
+
+                @pl.when(core == 0)
+                def _():
+                    send_rest(m)
+    else:
+        pl.semaphore_wait(barrier, shards - 1)
         for d in range(1, shards):
-            lot = (pl.ds(g * span, span), pl.ds(d * cap, cap))
-            remote(send.at[lot], recv.at[lot], row_ssem.at[0], row_rsem.at[g], peer(d)).start()
-
-    def rows_in(g):
-        lot = (pl.ds(g * span, span), pl.ds(cap, slots - cap))
-        return all_of(recv.at[lot], row_ssem.at[0], row_rsem.at[g])
-
-    @pl.when(core == 0)
-    def _():
-        attend_new()
+            send_meta(d)
+        for c in range(len(chunks)):
+            for d in range(1, shards):
+                send_rows(c, d)
+
+        @pl.when(core == 0)
+        def _():
+            attend_new()
 
     meta_in = all_of(meta_recv.at[others], meta_sem.at[0], meta_sem.at[1])
     meta_in.wait_recv()
@@ -198,15 +282,21 @@
 
     def merge(i):
         r, h = divmod(i, heads)
-        if i == 0:
-            load.wait()
-        if i % span == 0:
-            rows_in(i // span).wait_recv()
         placing = jnp.where(
             kept_row == slot_position[i : i + 1], slot_weight[i : i + 1], 0.0
         ).astype(BF16)
+        factor = 1.0 / (1.0 + jnp.dot(placing, ones, preferred_element_type=F32))
+        if i == 0:
+            load.wait()
+        for c, (first, _) in enumerate(chunks):
+            if first == i:
+                rows_in(c).wait_recv()
+        if chain and i == 0:
+            for m in range(shards):
+                @pl.when((me == m) & (core != 0))
+                def _():
+                    send_rest(m)
         summed = jnp.dot(placing, recv[i], preferred_element_type=F32)
-        factor = 1.0 / (1.0 + jnp.dot(placing, ones, preferred_element_type=F32))
         factor = jnp.concatenate([factor] * (width // 128), axis=1)
         fused = ((merged[r, h].astype(F32) + summed) * factor).astype(BF16)
         merged[r, h] = fused
@@ -219,20 +309,20 @@
         away = lax.rem(owner - me + shards, shards)
         return (
             remote(
-                part.at[k, lot], part_recv.at[k, away, lot],
-                part_ssem.at[k, 0], part_rsem.at[k, 0], owner,
+                part.at[k, lot], part_recv.at[0, away, lot],
+                part_ssem.at[k, 0], part_rsem.at[0, 0], owner,
             ),
             remote(
-                part_m.at[k], part_m_recv.at[k, away],
-                part_ssem.at[k, 1], part_rsem.at[k, 1], owner,
+                part_m.at[k], part_m_recv.at[0, away],
+                part_ssem.at[k, 1], part_rsem.at[0, 1], owner,
             ),
         )
 
     def parts_in(k, count):
         lot = pl.ds(0, count * rows)
         return (
-            all_of(part_recv.at[k, others, lot], part_ssem.at[k, 0], part_rsem.at[k, 0]),
-            all_of(part_m_recv.at[k, others], part_ssem.at[k, 1], part_rsem.at[k, 1]),
+            all_of(part_recv.at[0, others, lot], part_ssem.at[k, 0], part_rsem.at[0, 0]),
+            all_of(part_m_recv.at[0, others], part_ssem.at[k, 1], part_rsem.at[0, 1]),
         )
 
     def share_rows(k, j, d):
@@ -252,7 +342,7 @@
 
     def send_result(k, first, count, d):
         lot = result.at[pl.ds(first, count)]
-        return remote(lot, lot, res_ssem.at[k], res_rsem.at[k], peer(d))
+        return remote(lot, lot, res_ssem.at[0], res_rsem.at[k], peer(d))
 
     owned_plan = [(k, *entry) for k, entry in enumerate(plan) if entry[2] is not None]
     owned_index = {entry[0]: n for n, entry in enumerate(owned_plan)}
@@ -314,7 +404,7 @@
             combine(
                 first, count,
                 [(part.at[n], part_m.at[n])]
-                + [(part_recv.at[n, d], part_m_recv.at[n, d]) for d in range(1, shards)],
+                + [(part_recv.at[0, d], part_m_recv.at[0, d]) for d in range(1, shards)],
             )
             for d in range(1, shards):
                 send_result(n, first, count, d).start()
@@ -350,8 +440,8 @@
 
         @pl.when(me == owner)
         def _():
-            lot = part_recv.at[n, others, pl.ds(0, count * rows)]
-            all_of(lot, res_ssem.at[n], res_rsem.at[n]).wait_send()
+            lot = part_recv.at[0, others, pl.ds(0, count * rows)]
+            all_of(lot, res_ssem.at[0], res_rsem.at[n]).wait_send()
 
     for k, first, count, _ in shared_plan:
         for copy in shares(shared_index[k], count):
@@ -372,13 +462,17 @@
 def schedule(shards, pairs):
     per = max(1, pairs // shards)
     firsts = list(range(0, pairs, per))
-    late = len(firsts) // 2 if shards <= 8 else 0
-    return tuple(
-        (first, min(per, pairs - first), None)
-        if n >= len(firsts) - late
-        else (first, min(per, pairs - first), (shards // 2 - 1 + n) % shards)
-        for n, first in enumerate(firsts)
-    )
+    owners = [(shards - 2 - n) % shards if shards <= 8 else n % shards for n in range(len(firsts))]
+    if shards <= 8:
+        owners[-1] = None
+    return tuple((f, min(per, pairs - f), owner) for f, owner in zip(firsts, owners))
+
+
+def row_chunks(shards, pairs):
+    if shards > 8 or shards < 3:
+        return ((0, pairs),)
+    head = max(1, 3 * pairs // 8)
+    return ((0, head),) + tuple((i, 1) for i in range(head, pairs))
 
 
 def body(shards, cache, evicted, merge_weight, targets, kept_counts, queries, new_rows):
@@ -389,7 +483,7 @@
     rows = steps * query_local // heads
     cap = -(-max(2, 2 * evict // shards) // 16) * 16
     slots = shards * cap
-    groups = pairs if shards <= 8 else 1
+    chunks = row_chunks(shards, pairs)
     plan = schedule(shards, pairs)
     most = max(count for _, count, _ in plan)
     owned = max(1, sum(owner is not None for _, _, owner in plan))
@@ -397,7 +491,7 @@
     high = -(-3 * most // 8) * 8
     dma = pltpu.SemaphoreType.DMA
     done = pl.pallas_call(
-        functools.partial(kernel, shards, cap, groups, plan),
+        functools.partial(kernel, shards, cap, chunks, plan),
         out_shape=(
             jax.ShapeDtypeStruct(cache.shape, BF16),
             jax.ShapeDtypeStruct(queries.shape, BF16),
@@ -420,21 +514,22 @@
             pltpu.VMEM((pairs, 8, 128), F32),
             pltpu.VMEM((owned, most * rows, depth), jnp.int16),
             pltpu.VMEM((owned, high, 128), F32),
-            pltpu.VMEM((owned, shards, most * rows, depth), jnp.int16),
-            pltpu.VMEM((owned, shards, high, 128), F32),
+            pltpu.VMEM((1, shards, most * rows, depth), jnp.int16),
+            pltpu.VMEM((1, shards, high, 128), F32),
             pltpu.VMEM((common, shards, most * rows, depth), jnp.int16),
             pltpu.VMEM((common, shards, high, 128), F32),
             pltpu.VMEM((pairs, rows, depth), BF16),
+            pltpu.SemaphoreType.REGULAR((2, max(1, shards - 2))),
             dma((6,)),
             dma((1,)),
             dma((1,)),
-            dma((groups,)),
+            dma((len(chunks),)),
             dma((2,)),
             dma((owned, 2)),
-            dma((owned, 2)),
+            dma((1, 2)),
             dma((common, 2)),
             dma((common, 2)),
-            dma((owned,)),
+            dma((1,)),
             dma((owned,)),
         ],
         compiler_params=pltpu.CompilerParams(

time: 26.5 us -> 24.9 us (0.940)
  Pallas kernels: 25.7 us -> 24.1 us
    pallas_call x1, Pallas kernels: 24.5 us -> 22.9 us  [body(): pl.pallas_call(functools.partial(kernel, shards, cap, chunks, plan), out_...]
where the time goes in v3:
time: 24.9 us; the launch traced here: 24.7 us
  Pallas kernels  24.1 us (97%)
  between operations  0.64 us (3%)
    pallas_call x1, Pallas kernels, body(): pl.pallas_call(functools.partial(kernel, shards, cap, chunks, plan), out_...  22.9 us
    pallas_call x1, Pallas kernels, body(): pl.pallas_call(write_out, out_shape=tuple((jax.ShapeDtypeStruct(a.shape,...  1.17 us

profile of v3, /device:TPU:0, one launch (start us, length us, event | category | flops | bytes accessed | tf_op | source)
XLA Modules:
  0.0 24.7 jit_solution(11686833077031368838)
XLA Ops:
  0.6 22.9 %shard_map.86 = (bf16[2,4,384,256]{3,2,1,0:T(8,128)(2,1)S(1)}, bf16[4,2,32,128]{3,2,1,0:T(8,128)(2,1)S(1)}) custom-call(bf16[2,4,384,256]{3,2,1,0:T(8,128)(2,1)} %cache.1, bf16[2,4,64,256]{3,2,1,0:T(8,128)(2,1)} %evicted.1, bf16[2,4,64]{2,1,0:T(4,128)(2,1)} %weight.1, s32[2,4,64]{2,1,0:T(4,128)} %target.1, s32[1,2]{1,0:T(1,128)} %bitcast.1, ...), custom_call_target="tpu_custom_call" | custom-call | tf_op jit(solution)/shard_map/pallas_call | solution.py:493
  23.6 1.2 %shard_map.87 = (bf16[2,4,384,256]{3,2,1,0:T(8,128)(2,1)}, bf16[4,2,32,128]{3,2,1,0:T(8,128)(2,1)}) custom-call(bf16[2,4,384,256]{3,2,1,0:T(8,128)(2,1)S(1)} %get-tuple-element.4.merged, bf16[4,2,32,128]{3,2,1,0:T(8,128)(2,1)S(1)} %get-tuple-element.5.attended), custom_call_target="tpu_custom_call" | custom-call | tf_op jit(solution)/shard_map/pallas_call | solution.py:542

commit v4 on v3

--- a/solution.py
+++ b/solution.py
@@ -90,16 +90,19 @@
         for d in range(1, shards):
             tell(barrier, peer(d))
 
-    diagonal = lax.broadcasted_iota(jnp.int32, (rows, 128), 0) == lax.broadcasted_iota(
-        jnp.int32, (rows, 128), 1
+    ahead = lax.broadcasted_iota(jnp.int32, (rows, 128), 1) - lax.broadcasted_iota(
+        jnp.int32, (rows, 128), 0
     )
-
-    def to_rows(*columns):
-        flat = [jnp.sum(jnp.where(diagonal, c, 0.0), axis=0, keepdims=True) for c in columns]
-        return jnp.concatenate(flat, axis=0)
-
-    def to_column(row):
-        return jnp.sum(jnp.where(diagonal, row, 0.0), axis=1, keepdims=True)
+    spot = {first + j: j * rows for first, count, _ in plan for j in range(count)}
+
+    def to_row(*placed):
+        grid = jnp.zeros((rows, 128), F32)
+        for column, at in placed:
+            grid = jnp.where(ahead == at, column, grid)
+        return jnp.sum(grid, axis=0, keepdims=True)
+
+    def to_column(row, at):
+        return jnp.sum(jnp.where(ahead == at, row, 0.0), axis=1, keepdims=True)
 
     def attend_new():
         padded = -(-steps // 16) * 16
@@ -125,7 +128,8 @@
                     query, latest[:, :depth], latest[:, depth:], allowed, scale
                 )
                 fresh_o[i] = weighted
-                fresh_ml[i, 0:2, :] = to_rows(highest, total)
+                fresh_ml[i, 0:1, :] = to_row((highest, spot[i]))
+                fresh_ml[i, 1:2, :] = to_row((total, spot[i]))
 
     for copy in small[3:]:
         copy.wait()
@@ -276,15 +280,19 @@
     slot_position = (meta * (1.0 / 2048.0)).astype(jnp.int32)
     slot_weight = (meta - slot_position.astype(F32) * 2048.0) * (1.0 / 512.0)
 
-    kept_row = lax.broadcasted_iota(jnp.int32, (kept, slots), 0)
+    kept_row = lax.broadcasted_iota(jnp.int32, (kept, slots), 0).astype(jnp.int16)
     kept_lane = lax.broadcasted_iota(jnp.int32, (rows, kept), 1)
     ones = jnp.ones((slots, 128), BF16)
 
     def merge(i):
         r, h = divmod(i, heads)
+        aims = jnp.broadcast_to(slot_position[i : i + 1], (16, slots)).astype(jnp.int16)
+        gains = jnp.broadcast_to(slot_weight[i : i + 1], (16, slots)).astype(BF16)
         placing = jnp.where(
-            kept_row == slot_position[i : i + 1], slot_weight[i : i + 1], 0.0
-        ).astype(BF16)
+            kept_row == jnp.concatenate([aims] * (kept // 16), axis=0),
+            jnp.concatenate([gains] * (kept // 16), axis=0),
+            jnp.zeros((kept, slots), BF16),
+        )
         factor = 1.0 / (1.0 + jnp.dot(placing, ones, preferred_element_type=F32))
         if i == 0:
             load.wait()
@@ -350,6 +358,7 @@
     shared_index = {entry[0]: n for n, entry in enumerate(shared_plan)}
 
     for k, (first, count, owner) in enumerate(plan):
+        tops, sums = [], []
         for j in range(count):
             highest, total, weighted = merge(first + j)
             size = jnp.maximum(jnp.max(jnp.abs(weighted), axis=-1, keepdims=True), 1e-30)
@@ -362,7 +371,11 @@
             if owner is None:
                 for d in range(1, shards):
                     share_rows(shared_index[k], j, d).start()
-            into_m[3 * j : 3 * j + 3, :] = to_rows(highest, total, size * (1.0 / 32767.0))
+            at = j * rows
+            tops.append(to_row((highest, at), (size * (1.0 / 32767.0), at + 64)))
+            sums.append(to_row((total, at)))
+        into_m[0:1, :] = functools.reduce(jnp.add, tops)
+        into_m[1:2, :] = functools.reduce(jnp.add, sums)
         if owner is None:
             for d in range(1, shards):
                 share_tops(shared_index[k], d).start()
@@ -375,23 +388,25 @@
     lanes = lax.broadcasted_iota(jnp.int32, (1, 128), 1)
 
     def combine(first, count, blocks):
-        for j in range(count):
-            i = first + j
-            tiles = [fresh_ml[i, 0:2, :]] + [m[3 * j : 3 * j + 3, :] for _, m in blocks]
-            outs = [fresh_o[i]] + [
-                b[j * rows : (j + 1) * rows, :].astype(jnp.int32).astype(F32) for b, _ in blocks
-            ]
-            top = tiles[0][0:1]
-            for tile in tiles[1:]:
-                top = jnp.maximum(top, tile[0:1])
-            shares = [jnp.exp(tile[0:1] - top) for tile in tiles]
-            total = shares[0] * tiles[0][1:2]
-            for share, tile in zip(shares[1:], tiles[1:]):
-                total = total + share * tile[1:2]
-            total = jnp.where(lanes < rows, total, 1.0)
-            blend = to_column(shares[0] / total) * outs[0]
-            for share, tile, out in zip(shares[1:], tiles[1:], outs[1:]):
-                blend = blend + to_column(share * tile[2:3] / total) * out
+        group = range(first, first + count)
+        tiles = [
+            (
+                functools.reduce(jnp.add, [fresh_ml[i, 0:1, :] for i in group]),
+                functools.reduce(jnp.add, [fresh_ml[i, 1:2, :] for i in group]),
+            )
+        ] + [(m[0:1, :], m[1:2, :]) for _, m in blocks]
+        top = functools.reduce(jnp.maximum, [tile[0] for tile in tiles])
+        shares = [jnp.exp(tile[0] - top) for tile in tiles]
+        total = functools.reduce(jnp.add, [a * tile[1] for a, tile in zip(shares, tiles)])
+        shares = [a / jnp.where(lanes < count * rows, total, 1.0) for a in shares]
+        for n, (_, m) in enumerate(blocks):
+            scales = jnp.concatenate([m[0:1, 64:], m[0:1, :64]], axis=1)
+            shares[n + 1] = shares[n + 1] * scales
+        for j, i in enumerate(group):
+            blend = to_column(shares[0], j * rows) * fresh_o[i]
+            for share, (b, _) in zip(shares[1:], blocks):
+                out = b[j * rows : (j + 1) * rows, :].astype(jnp.int32).astype(F32)
+                blend = blend + to_column(share, j * rows) * out
             result[i] = blend.astype(BF16)
 
     for k, first, count, owner in owned_plan:
@@ -460,7 +475,7 @@
 
 
 def schedule(shards, pairs):
-    per = max(1, pairs // shards)
+    per = max(1, min(2, pairs // shards))
     firsts = list(range(0, pairs, per))
     owners = [(shards - 2 - n) % shards if shards <= 8 else n % shards for n in range(len(firsts))]
     if shards <= 8:
@@ -488,7 +503,8 @@
     most = max(count for _, count, _ in plan)
     owned = max(1, sum(owner is not None for _, _, owner in plan))
     common = max(1, len(plan) - owned)
-    high = -(-3 * most // 8) * 8
+    assert most * rows <= 64
+    high = 2
     dma = pltpu.SemaphoreType.DMA
     done = pl.pallas_call(
         functools.partial(kernel, shards, cap, chunks, plan),
@@ -511,7 +527,7 @@
             pltpu.VMEM((shards, pairs, slots), F32),
             pltpu.VMEM((pairs, rows, depth), BF16),
             pltpu.VMEM((pairs, rows, depth), F32),
-            pltpu.VMEM((pairs, 8, 128), F32),
+            pltpu.VMEM((pairs, 2, 128), F32),
             pltpu.VMEM((owned, most * rows, depth), jnp.int16),
             pltpu.VMEM((owned, high, 128), F32),
             pltpu.VMEM((1, shards, most * rows, depth), jnp.int16),

time: 24.9 us -> 24.8 us (level)
  no operation moved by 1% of the time
where the time goes in v4:
time: 24.8 us; the launch traced here: 24.6 us
  Pallas kernels  24 us (97%)
  between operations  0.64 us (3%)
    pallas_call x1, Pallas kernels, body(): pl.pallas_call(functools.partial(kernel, shards, cap, chunks, plan), out_...  22.8 us
    pallas_call x1, Pallas kernels, body(): pl.pallas_call(write_out, out_shape=tuple((jax.ShapeDtypeStruct(a.shape,...  1.17 us

profile of v4, /device:TPU:0, one launch (start us, length us, event | category | flops | bytes accessed | tf_op | source)
XLA Modules:
  0.0 24.6 jit_solution(6622048973660209215)
XLA Ops:
  0.6 22.8 %shard_map.86 = (bf16[2,4,384,256]{3,2,1,0:T(8,128)(2,1)S(1)}, bf16[4,2,32,128]{3,2,1,0:T(8,128)(2,1)S(1)}) custom-call(bf16[2,4,384,256]{3,2,1,0:T(8,128)(2,1)} %cache.1, bf16[2,4,64,256]{3,2,1,0:T(8,128)(2,1)} %evicted.1, bf16[2,4,64]{2,1,0:T(4,128)(2,1)} %weight.1, s32[2,4,64]{2,1,0:T(4,128)} %target.1, s32[1,2]{1,0:T(1,128)} %bitcast.1, ...), custom_call_target="tpu_custom_call" | custom-call | tf_op jit(solution)/shard_map/pallas_call | solution.py:509
  23.5 1.2 %shard_map.87 = (bf16[2,4,384,256]{3,2,1,0:T(8,128)(2,1)}, bf16[4,2,32,128]{3,2,1,0:T(8,128)(2,1)}) custom-call(bf16[2,4,384,256]{3,2,1,0:T(8,128)(2,1)S(1)} %get-tuple-element.4.merged, bf16[4,2,32,128]{3,2,1,0:T(8,128)(2,1)S(1)} %get-tuple-element.5.attended), custom_call_target="tpu_custom_call" | custom-call | tf_op jit(solution)/shard_map/pallas_call | solution.py:558

commit v5 on v4

--- a/solution.py
+++ b/solution.py
@@ -59,6 +59,23 @@
             device_id={"seq": device}, device_id_type=pl.DeviceIdType.MESH,
         )
 
+    def tell(sem, device):
+        pl.semaphore_signal(
+            sem, inc=1, device_id={"seq": device}, device_id_type=pl.DeviceIdType.MESH
+        )
+
+    chain = len(chunks) > 1
+    barrier = pltpu.get_barrier_semaphore()
+    if chain:
+        for m in range(shards):
+            @pl.when(me == m)
+            def _():
+                for t in [m - 1] * (m > 0) + list(range(m + 1, shards)):
+                    tell(barrier, t)
+    else:
+        for d in range(1, shards):
+            tell(barrier, peer(d))
+
     small = [
         pltpu.make_async_copy(src, dst, in_sem.at[i])
         for i, (src, dst) in enumerate((
@@ -70,25 +87,6 @@
         copy.start()
     load = pltpu.make_async_copy(cache, merged, cache_sem.at[0])
     load.start()
-
-    def tell(sem, device):
-        pl.semaphore_signal(
-            sem, inc=1, device_id={"seq": device}, device_id_type=pl.DeviceIdType.MESH
-        )
-
-    chain = len(chunks) > 1
-    barrier = pltpu.get_barrier_semaphore()
-    if chain:
-        @pl.when(me > 0)
-        def _():
-            tell(barrier, me - 1)
-
-        @pl.when(me < shards - 1)
-        def _():
-            tell(barrier, me + 1)
-    else:
-        for d in range(1, shards):
-            tell(barrier, peer(d))
 
     ahead = lax.broadcasted_iota(jnp.int32, (rows, 128), 1) - lax.broadcasted_iota(
         jnp.int32, (rows, 128), 0
@@ -210,25 +208,16 @@
         pack(i)
 
     if chain:
-        inner = (me > 0) & (me < shards - 1)
-
-        @pl.when(jnp.logical_not(inner))
-        def _():
-            pl.semaphore_wait(barrier, 1)
-
-        @pl.when(inner)
-        def _():
-            pl.semaphore_wait(barrier, 2)
-            tell(near_sem.at[0, 0], me - 1)
-            tell(near_sem.at[1, 0], me + 1)
-
-        @pl.when(me < shards - 1)
-        def _():
-            send_rows(0, 1)
-
-        @pl.when(me > 0)
-        def _():
-            send_rows(0, shards - 1)
+        for m in range(shards):
+            @pl.when(me == m)
+            def _():
+                pl.semaphore_wait(barrier, m + (m < shards - 1))
+                if 0 < m < shards - 1:
+                    tell(near_sem.at[0], m - 1)
+                for t in range(m):
+                    send_rows(0, (t - m) % shards)
+                if m < shards - 1:
+                    send_rows(0, 1)
 
     for i in range(chunks[0][1], pairs):
         pack(i)
@@ -241,17 +230,11 @@
         for m in range(shards):
             @pl.when(me == m)
             def _():
-                for far in range(2, shards):
-                    if m + far < shards:
-                        pl.semaphore_wait(near_sem.at[0, far - 2], 1)
-                        if m > 0:
-                            tell(near_sem.at[0, far - 1], m - 1)
-                        send_rows(0, far)
-                    if m - far >= 0:
-                        pl.semaphore_wait(near_sem.at[1, far - 2], 1)
-                        if m < shards - 1:
-                            tell(near_sem.at[1, far - 1], m + 1)
-                        send_rows(0, shards - far)
+                for far in range(2, shards - m):
+                    pl.semaphore_wait(near_sem.at[far - 2], 1)
+                    if m > 0:
+                        tell(near_sem.at[far - 1], m - 1)
+                    send_rows(0, far)
                 there = sorted((t for t in range(shards) if t != m), key=lambda t: -abs(t - m))
                 for t in there:
                     send_meta((t - m) % shards)
@@ -477,10 +460,13 @@
 def schedule(shards, pairs):
     per = max(1, min(2, pairs // shards))
     firsts = list(range(0, pairs, per))
-    owners = [(shards - 2 - n) % shards if shards <= 8 else n % shards for n in range(len(firsts))]
-    if shards <= 8:
-        owners[-1] = None
-    return tuple((f, min(per, pairs - f), owner) for f, owner in zip(firsts, owners))
+    near = shards <= 8
+    late = len(firsts) // 2 if near else 0
+    plan = []
+    for n, first in enumerate(firsts):
+        owner = (shards // 2 - 1 + n) % shards if near else n % shards
+        plan.append((first, min(per, pairs - first), owner if n < len(firsts) - late else None))
+    return tuple(plan)
 
 
 def row_chunks(shards, pairs):
@@ -535,7 +521,7 @@
             pltpu.VMEM((common, shards, most * rows, depth), jnp.int16),
             pltpu.VMEM((common, shards, high, 128), F32),
             pltpu.VMEM((pairs, rows, depth), BF16),
-            pltpu.SemaphoreType.REGULAR((2, max(1, shards - 2))),
+            pltpu.SemaphoreType.REGULAR((max(1, shards - 2),)),
             dma((6,)),
             dma((1,)),
             dma((1,)),

time: 24.8 us -> 24.6 us (level)
  no operation moved by 1% of the time
where the time goes in v5:
time: 24.6 us; the launch traced here: 24.4 us
  Pallas kernels  23.8 us (97%)
  between operations  0.64 us (3%)
    pallas_call x1, Pallas kernels, body(): pl.pallas_call(functools.partial(kernel, shards, cap, chunks, plan), out_...  22.6 us
    pallas_call x1, Pallas kernels, body(): pl.pallas_call(write_out, out_shape=tuple((jax.ShapeDtypeStruct(a.shape,...  1.17 us

profile of v5, /device:TPU:0, one launch (start us, length us, event | category | flops | bytes accessed | tf_op | source)
XLA Modules:
  0.0 24.4 jit_solution(11059574735027244794)
XLA Ops:
  0.6 22.6 %shard_map.86 = (bf16[2,4,384,256]{3,2,1,0:T(8,128)(2,1)S(1)}, bf16[4,2,32,128]{3,2,1,0:T(8,128)(2,1)S(1)}) custom-call(bf16[2,4,384,256]{3,2,1,0:T(8,128)(2,1)} %cache.1, bf16[2,4,64,256]{3,2,1,0:T(8,128)(2,1)} %evicted.1, bf16[2,4,64]{2,1,0:T(4,128)(2,1)} %weight.1, s32[2,4,64]{2,1,0:T(4,128)} %target.1, s32[1,2]{1,0:T(1,128)} %bitcast.1, ...), custom_call_target="tpu_custom_call" | custom-call | tf_op jit(solution)/shard_map/pallas_call | solution.py:495
  23.3 1.2 %shard_map.87 = (bf16[2,4,384,256]{3,2,1,0:T(8,128)(2,1)}, bf16[4,2,32,128]{3,2,1,0:T(8,128)(2,1)}) custom-call(bf16[2,4,384,256]{3,2,1,0:T(8,128)(2,1)S(1)} %get-tuple-element.4.merged, bf16[4,2,32,128]{3,2,1,0:T(8,128)(2,1)S(1)} %get-tuple-element.5.attended), custom_call_target="tpu_custom_call" | custom-call | tf_op jit(solution)/shard_map/pallas_call | solution.py:544

commit v6 on v5

--- a/solution.py
+++ b/solution.py
@@ -194,14 +194,14 @@
         lot = (pl.ds(first, count), pl.ds(cap, slots - cap))
         return all_of(recv.at[lot], row_ssem.at[0], row_rsem.at[c])
 
-    def send_rest(m):
+    def send_rest(m, low, high):
         there = sorted((t for t in range(shards) if t != m), key=lambda t: -abs(t - m))
         edge = m in (0, shards - 1)
-        for c in range(1, len(chunks)):
+        for c in range(low, high):
             for t in there[:-1] if edge else there:
                 send_rows(c, (t - m) % shards)
         if edge:
-            for c in range(1, len(chunks)):
+            for c in range(low, high):
                 send_rows(c, (there[-1] - m) % shards)
 
     for i in range(chunks[0][1]):
@@ -239,9 +239,11 @@
                 for t in there:
                     send_meta((t - m) % shards)
 
+                keep = 0 if 0 < m < shards - 1 else 1
+
                 @pl.when(core == 0)
                 def _():
-                    send_rest(m)
+                    send_rest(m, 1, len(chunks) - keep)
     else:
         pl.semaphore_wait(barrier, shards - 1)
         for d in range(1, shards):
@@ -286,7 +288,13 @@
             for m in range(shards):
                 @pl.when((me == m) & (core != 0))
                 def _():
-                    send_rest(m)
+                    send_rest(m, 1, len(chunks))
+
+                keep = 0 if 0 < m < shards - 1 else 1
+                if keep:
+                    @pl.when((me == m) & (core == 0))
+                    def _():
+                        send_rest(m, len(chunks) - keep, len(chunks))
         summed = jnp.dot(placing, recv[i], preferred_element_type=F32)
         factor = jnp.concatenate([factor] * (width // 128), axis=1)
         fused = ((merged[r, h].astype(F32) + summed) * factor).astype(BF16)

time: 24.6 us -> 24.5 us (level)
  Pallas kernels: 23.8 us -> 23.5 us
    pallas_call x1, Pallas kernels: 22.6 us -> 22.3 us  [body(): pl.pallas_call(functools.partial(kernel, shards, cap, chunks, plan), out_...]
where the time goes in v6:
time: 24.5 us; the launch traced here: 24.1 us
  Pallas kernels  23.5 us (96%)
  between operations  0.64 us (3%)
    pallas_call x1, Pallas kernels, body(): pl.pallas_call(functools.partial(kernel, shards, cap, chunks, plan), out_...  22.3 us
    pallas_call x1, Pallas kernels, body(): pl.pallas_call(write_out, out_shape=tuple((jax.ShapeDtypeStruct(a.shape,...  1.17 us

profile of v6, /device:TPU:0, one launch (start us, length us, event | category | flops | bytes accessed | tf_op | source)
XLA Modules:
  0.0 24.1 jit_solution(7017934121069359122)
XLA Ops:
  0.6 22.3 %shard_map.86 = (bf16[2,4,384,256]{3,2,1,0:T(8,128)(2,1)S(1)}, bf16[4,2,32,128]{3,2,1,0:T(8,128)(2,1)S(1)}) custom-call(bf16[2,4,384,256]{3,2,1,0:T(8,128)(2,1)} %cache.1, bf16[2,4,64,256]{3,2,1,0:T(8,128)(2,1)} %evicted.1, bf16[2,4,64]{2,1,0:T(4,128)(2,1)} %weight.1, s32[2,4,64]{2,1,0:T(4,128)} %target.1, s32[1,2]{1,0:T(1,128)} %bitcast.1, ...), custom_call_target="tpu_custom_call" | custom-call | tf_op jit(solution)/shard_map/pallas_call | solution.py:503
  22.9 1.2 %shard_map.87 = (bf16[2,4,384,256]{3,2,1,0:T(8,128)(2,1)}, bf16[4,2,32,128]{3,2,1,0:T(8,128)(2,1)}) custom-call(bf16[2,4,384,256]{3,2,1,0:T(8,128)(2,1)S(1)} %get-tuple-element.4.merged, bf16[4,2,32,128]{3,2,1,0:T(8,128)(2,1)S(1)} %get-tuple-element.5.attended), custom_call_target="tpu_custom_call" | custom-call | tf_op jit(solution)/shard_map/pallas_call | solution.py:552

commit v7 on v6

--- a/solution.py
+++ b/solution.py
@@ -326,17 +326,17 @@
 
     def share_rows(k, j, d):
         lot = shared.at[k, me, pl.ds(j * rows, rows)]
-        return remote(lot, lot, share_ssem.at[k, 0], share_rsem.at[k, 0], peer(d))
+        return remote(lot, lot, share_ssem.at[0], share_rsem.at[k, 0], peer(d))
 
     def share_tops(k, d):
         lot = shared_m.at[k, me]
-        return remote(lot, lot, share_ssem.at[k, 1], share_rsem.at[k, 1], peer(d))
+        return remote(lot, lot, share_ssem.at[1], share_rsem.at[k, 1], peer(d))
 
     def shares(k, count):
         lot = pl.ds(0, count * rows)
         return (
-            all_of(shared.at[k, others, lot], share_ssem.at[k, 0], share_rsem.at[k, 0]),
-            all_of(shared_m.at[k, others], share_ssem.at[k, 1], share_rsem.at[k, 1]),
+            all_of(shared.at[k, others, lot], share_ssem.at[0], share_rsem.at[k, 0]),
+            all_of(shared_m.at[k, others], share_ssem.at[1], share_rsem.at[k, 1]),
         )
 
     def send_result(k, first, count, d):
@@ -449,9 +449,11 @@
             lot = part_recv.at[0, others, pl.ds(0, count * rows)]
             all_of(lot, res_ssem.at[0], res_rsem.at[n]).wait_send()
 
-    for k, first, count, _ in shared_plan:
-        for copy in shares(shared_index[k], count):
-            copy.wait_send()
+    if shared_plan:
+        gone = (pl.ds(0, len(shared_plan)), others)
+        lot = (*gone, pl.ds(0, shared_plan[0][2] * rows))
+        all_of(shared.at[lot], share_ssem.at[0], share_rsem.at[0, 0]).wait_send()
+        all_of(shared_m.at[gone], share_ssem.at[1], share_rsem.at[0, 1]).wait_send()
 
 
 def write_out(merged, attended, merged_out, attended_out, sem):
@@ -537,7 +539,7 @@
             dma((2,)),
             dma((owned, 2)),
             dma((1, 2)),
-            dma((common, 2)),
+            dma((2,)),
             dma((common, 2)),
             dma((1,)),
             dma((owned,)),

time: 24.5 us -> 24.5 us (level)
  no operation moved by 1% of the time
where the time goes in v7:
time: 24.5 us; the launch traced here: 24.1 us
  Pallas kernels  23.5 us (96%)
  between operations  0.64 us (3%)
    pallas_call x1, Pallas kernels, body(): pl.pallas_call(functools.partial(kernel, shards, cap, chunks, plan), out_...  22.3 us
    pallas_call x1, Pallas kernels, body(): pl.pallas_call(write_out, out_shape=tuple((jax.ShapeDtypeStruct(a.shape,...  1.17 us

profile of v7, /device:TPU:0, one launch (start us, length us, event | category | flops | bytes accessed | tf_op | source)
XLA Modules:
  0.0 24.1 jit_solution(11906877026893706712)
XLA Ops:
  0.6 22.3 %shard_map.86 = (bf16[2,4,384,256]{3,2,1,0:T(8,128)(2,1)S(1)}, bf16[4,2,32,128]{3,2,1,0:T(8,128)(2,1)S(1)}) custom-call(bf16[2,4,384,256]{3,2,1,0:T(8,128)(2,1)} %cache.1, bf16[2,4,64,256]{3,2,1,0:T(8,128)(2,1)} %evicted.1, bf16[2,4,64]{2,1,0:T(4,128)(2,1)} %weight.1, s32[2,4,64]{2,1,0:T(4,128)} %target.1, s32[1,2]{1,0:T(1,128)} %bitcast.1, ...), custom_call_target="tpu_custom_call" | custom-call | tf_op jit(solution)/shard_map/pallas_call | solution.py:505
  22.9 1.2 %shard_map.87 = (bf16[2,4,384,256]{3,2,1,0:T(8,128)(2,1)}, bf16[4,2,32,128]{3,2,1,0:T(8,128)(2,1)}) custom-call(bf16[2,4,384,256]{3,2,1,0:T(8,128)(2,1)S(1)} %get-tuple-element.4.merged, bf16[4,2,32,128]{3,2,1,0:T(8,128)(2,1)S(1)} %get-tuple-element.5.attended), custom_call_target="tpu_custom_call" | custom-call | tf_op jit(solution)/shard_map/pallas_call | solution.py:554
